TPU v7x, 32 devices: a whole 2x2x4 slice. The times are simulated.
32 devices in a mesh: space: 8 (over z, y), rep: 4 (over x, core).
Axes of the slice: x: 2, y: 2, z: 4, core: 2. Of those that a mesh axis runs over, the one named last changes fastest.
Arguments:
- volumes: bfloat16 [4, 8, 8, 4, 16, 256], P('rep', 'space'), may hold values from -6 to 6
- grad_parts: bfloat16 [4, 2, 6912, 256], P('rep', None, 'space'), may hold values from -6 to 6
- master_weights: float32 [2, 6912, 256], P(None, 'space'), may hold values from -0.078125 to 0.078125
- moment_first: float32 [4, 2, 6912, 256], P('rep', None, 'space'), may hold values from -12 to 12
- moment_second: float32 [4, 2, 6912, 256], P('rep', None, 'space'), may hold values from 1 to 30
- owner: int32 [2, 32], replicated, may hold values from 0 to 3
Outputs:
- features: bfloat16 [4, 8, 8, 4, 16, 256], P('rep', 'space')
- new_weights: float32 [2, 1769472], P(None, ('space', 'rep'))
- moment_first_out: float32 [4, 2, 6912, 256], P('rep', None, 'space')
- moment_second_out: float32 [4, 2, 6912, 256], P('rep', None, 'space')
Inputs may be any that keep to these rules, and one draw needn't show every extreme that they name: owner[f, p] is the replica whose state slot holds the optimizer state of panel p of filter f, rows p * 216 to (p + 1) * 216 - 1; replicas may own unequal numbers of panels.
All inputs are finite; a program needn't handle non-finite values.
Results may differ from a plain program's by a relative error of at most 0.0095.
Values may be sent and summed in bfloat16 or wider, within the bound.
No kernel may reach another device: no remote copies, remote signals or barrier semaphores. Data moves between devices by JAX's collectives and lax.ppermute only.
A program may use at most 64 MiB of HBM per device.

v0:
```python
import jax
import jax.numpy as jnp
from jax import lax
from jax.sharding import PartitionSpec as P

GY = 2
GZ = 2
PANEL_ROWS = 216


def passed_along(value, axis, steps):
    count = lax.axis_size(axis)
    first, last = (max(0, -steps), min(count, count - steps))
    return lax.ppermute(value, axis, [(source, source + steps) for source in range(first, last)])


def spread(value, axis, source):
    kept = jnp.where(lax.axis_index(axis) == source, value, 0).astype(value.dtype)
    return lax.psum(kept, axis)


def neighbour(slab, offset):
    return passed_along(slab, "space", offset)


def keep_when(flag, slab):
    return jnp.where(flag, slab, jnp.zeros_like(slab))


def side_slab(array, dim, side):
    length = array.shape[dim]
    if side < 0:
        return lax.slice_in_dim(array, length - 1, length, 1, dim)
    return lax.slice_in_dim(array, 0, 1, 1, dim)


def extend_brick(brick, coords, strides, grid):
    lows = [coords[d] > 0 for d in range(3)]
    highs = [coords[d] < grid[d] - 1 for d in range(3)]
    current = brick
    for dim in range(3):
        lower = keep_when(lows[dim], neighbour(side_slab(current, dim, -1), strides[dim]))
        upper = keep_when(highs[dim], neighbour(side_slab(current, dim, 1), -strides[dim]))
        current = jnp.concatenate([lower, current, upper], axis=dim)
    return current


def convolve(extended, filter_rows):
    extent_x = extended.shape[0] - 2
    extent_y = extended.shape[1] - 2
    extent_z = extended.shape[2] - 2
    channels = extended.shape[3]
    summed = jnp.zeros((extent_x * extent_y * extent_z, filter_rows.shape[1]), jnp.float32)
    for shift_x in range(3):
        for shift_y in range(3):
            for shift_z in range(3):
                tap_index = (shift_x * 3 + shift_y) * 3 + shift_z
                window = extended[
                    shift_x : shift_x + extent_x,
                    shift_y : shift_y + extent_y,
                    shift_z : shift_z + extent_z,
                ]
                weights_tap = filter_rows[tap_index * channels : (tap_index + 1) * channels]
                summed = summed + jnp.dot(
                    window.reshape(-1, channels), weights_tap, preferred_element_type=jnp.float32
                )
    return summed.reshape(extent_x, extent_y, extent_z, -1)


def shards(volumes, grad_parts, master_weights, moment_first, moment_second, owner):
    filter_count = master_weights.shape[0]
    rows_dev = master_weights.shape[1]
    channels = master_weights.shape[2]
    panels_dev = rows_dev // PANEL_ROWS
    space_pos = lax.axis_index("space")
    rep_pos = lax.axis_index("rep")
    summed_grad = lax.psum(grad_parts[0].astype(jnp.float32).astype(jnp.bfloat16), "rep").astype(
        jnp.float32
    )
    first_new = 0.9 * moment_first[0] + 0.1 * summed_grad
    second_new = 0.95 * moment_second[0] + 0.05 * (summed_grad * summed_grad)
    owner_local = lax.dynamic_slice_in_dim(owner, space_pos * panels_dev, panels_dev, 1)
    owner_rows = jnp.repeat(owner_local, PANEL_ROWS, axis=1)
    owned = (owner_rows == rep_pos)[:, :, None]
    first_out = jnp.where(owned, first_new, moment_first[0])[None]
    second_out = jnp.where(owned, second_new, moment_second[0])[None]
    corr_one = 1.0 - 0.9**10
    corr_two = 1.0 - 0.95**10
    update = first_new / corr_one / (jnp.sqrt(second_new / corr_two) + 1e-08) + 0.1 * master_weights
    candidate = master_weights - 0.004 * update
    per_filter = []
    for filter_index in range(filter_count):
        slabs = []
        for panel_index in range(panels_dev):
            slab = candidate[
                filter_index, panel_index * PANEL_ROWS : (panel_index + 1) * PANEL_ROWS
            ]
            slabs.append(
                spread(
                    slab.astype(jnp.bfloat16), "rep", owner_local[filter_index, panel_index]
                ).astype(slab.dtype)
            )
        per_filter.append(jnp.concatenate(slabs, axis=0))
    new_master = jnp.stack(per_filter)
    share_len = rows_dev * channels // lax.axis_size("rep")
    new_weights = lax.dynamic_slice_in_dim(
        new_master.reshape(filter_count, -1), rep_pos * share_len, share_len, 1
    )
    filters = lax.all_gather(new_master.astype(jnp.bfloat16), "space", axis=1, tiled=True)
    grid = (lax.axis_size("space") // (GY * GZ), GY, GZ)
    strides = (GY * GZ, GZ, 1)
    coords = (space_pos // (GY * GZ), space_pos // GZ % GY, space_pos % GZ)
    brick = volumes[0, 0]
    hidden = jax.nn.gelu(
        convolve(extend_brick(brick, coords, strides, grid), filters[0]), approximate=True
    ).astype(jnp.bfloat16)
    output = jax.nn.gelu(
        convolve(extend_brick(hidden, coords, strides, grid), filters[1]), approximate=True
    ).astype(jnp.bfloat16)
    return (output[None, None], new_weights, first_out, second_out)


def solution(mesh):
    placed = (
        P("rep", "space", None, None, None, None),
        P("rep", None, "space", None),
        P(None, "space", None),
        P("rep", None, "space", None),
        P("rep", None, "space", None),
        P(),
    )
    return jax.shard_map(
        shards,
        mesh=mesh,
        in_specs=placed,
        out_specs=(
            P("rep", "space", None, None, None, None),
            P(None, ("space", "rep")),
            P("rep", None, "space", None),
            P("rep", None, "space", None),
        ),
        check_vma=False,
    )
```

profile of v0, /device:TPU:0, one launch (start us, length us, event | category | flops | bytes accessed | tf_op | source)
XLA Modules:
  0.0 271.1 jit_solution(5235828879841279045)
XLA Ops:
  14.8 34.0 %all-reduce.4.cloned.1.call-done = bf16[2,864,256]{2,1,0:T(8,128)(2,1)} async-done(((bf16[2,864,256]{2,1,0:T(8,128)(2,1)}), bf16[2,864,256]{2,1,0:T(8,128)(2,1)}) %all-reduce.4.cloned.1.call-update) | async-done | bytes 884752 | tf_op jit(solution)/shard_map/psum | solution.py:77
  48.7 4.8 %fusion.8 = (f32[1,2,864,256]{3,2,1,0:T(8,128)}, bf16[2,864,256]{2,1,0:T(8,128)(2,1)S(1)}, f32[1,2,864,256]{3,2,1,0:T(8,128)}) fusion(bf16[2,864,256]{2,1,0:T(8,128)(2,1)} %all-reduce.4.cloned.1.call-done, f32[1,2,864,256]{3,2,1,0:T(8,128)} %param.10, pred[2,864]{1,0:T(4,128)(4,1)S(1)} %eq.51, f32[2,864,256]{2,1,0:T(8,128)} %param.8, f32[1,2,864,256]{3,2,1,0:T(8,128)} %param.9), kind=kLoop, calls=%fused_computation.12 | loop fusion | flops 8404992 | bytes 10618560 | tf_op jit(solution)/shard_map/broadcast_in_dim | solution.py:86
  53.5 0.9 fusion.65
  54.5 36.1 %all-reduce.6.cloned.1.call-done = (bf16[216,256]{1,0:T(8,128)(2,1)}, bf16[216,256]{1,0:T(8,128)(2,1)}, bf16[216,256]{1,0:T(8,128)(2,1)}, bf16[216,256]{1,0:T(8,...) async-done(((bf16[216,256]{1,0:T(8,128)(2,1)}, bf16[216,256]{1,0:T(8,128)(2,1)}, ...) | async-done | bytes 884752 | tf_op jit(solution)/shard_map/psum | solution.py:19
  90.6 0.9 constant_dynamic-update-slice_fusion.7
  91.5 0.9 constant_dynamic-update-slice_fusion.3
  92.4 0.9 constant_dynamic-update-slice_fusion.6
  93.3 0.9 constant_dynamic-update-slice_fusion.5
  94.2 0.9 constant_dynamic-update-slice_fusion.2
  95.1 0.9 constant_dynamic-update-slice_fusion.1
  96.0 1.0 constant_dynamic-update-slice_fusion
  97.0 1.1 pad_maximum_fusion
  98.1 4.3 %collective-permute-start = (bf16[1,4,16,256]{3,2,1,0:T(8,128)(2,1)S(1)}, bf16[1,4,16,256]{3,2,1,0:T(8,128)(2,1)S(1)}, u32[]{:S(2)}, u32[]{:S(2)}) collective-permute-start(bf16[1,4,16,256]{3,2,1,0:T(8,128)(2,1)S(1)} %get-tuple-element.95), channel_id=1, source_target_pairs={{0,16},{4,20},{8,24},{12,28},{1,17},{5,21},{9,25},{13,29},{2,18},{... | collective-permute-start | bytes 98312 | tf_op jit(solution)/shard_map/ppermute | solution.py:14
  102.4 1.3 collective-permute-start.1
  104.0 5.1 %collective-permute-done.1 = bf16[1,4,16,256]{3,2,1,0:T(8,128)(2,1)S(1)} collective-permute-done((bf16[1,4,16,256]{3,2,1,0:T(8,128)(2,1)S(1)}, bf16[1,4,16,256]{3,2,1,0:T(8,128)(2,1)S(1)}, u32[]{:S(2)}, u32[]{:S(2)}) %collective-permute-start.1) | collective-permute-done | bytes 32800 | tf_op jit(solution)/shard_map/ppermute | solution.py:14
  109.2 3.4 %collective-permute-start.2 = (bf16[10,1,16,256]{3,2,1,0:T(8,128)(2,1)S(1)}, bf16[10,1,16,256]{3,2,1,0:T(8,128)(2,1)S(1)}, u32[]{:S(2)}, u32[]{:S(2)}) collective-permute-start(bf16[10,1,16,256]{3,2,1,0:T(8,128)(2,1)S(1)} %get-tuple-element.87), channel_id=1, source_target_pairs={{0,8},{4,12},{8,16},{12,20},{16,24},{20,28},{1,9},{5,13},{9,17},{1... | collective-permute-start | bytes 245768 | tf_op jit(solution)/shard_map/ppermute | solution.py:14
  112.6 1.3 collective-permute-start.3
  113.9 0.9 pad_maximum_fusion.7
  114.7 1.7 collective-permute-done.2
  116.4 6.2 %collective-permute-done.3 = bf16[10,1,16,256]{3,2,1,0:T(8,128)(2,1)S(1)} collective-permute-done((bf16[10,1,16,256]{3,2,1,0:T(8,128)(2,1)S(1)}, bf16[10,1,16,256]{3,2,1,0:T(8,128)(2,1)S(1)}, u32[]{:S(2)}, u32[]{:S(2)}) %collective-permute-start.3) | collective-permute-done | bytes 81952 | tf_op jit(solution)/shard_map/ppermute | solution.py:14
  122.7 3.4 %collective-permute-start.4 = (bf16[10,6,1,256]{3,2,1,0:T(2,128)(2,1)S(1)}, bf16[10,6,1,256]{3,2,1,0:T(2,128)(2,1)S(1)}, u32[]{:S(2)}, u32[]{:S(2)}) collective-permute-start(bf16[10,6,1,256]{3,2,1,0:T(2,128)(2,1)S(1)} %get-tuple-element.68), channel_id=1, source_target_pairs={{0,4},{4,8},{8,12},{12,16},{16,20},{20,24},{24,28},{1,5},{5,9},{9,... | collective-permute-start | bytes 92168 | tf_op jit(solution)/shard_map/ppermute | solution.py:14
  126.1 1.3 collective-permute-start.5
  127.5 1.1 fusion.79
  128.7 3.5 %collective-permute-done.5 = bf16[10,6,1,256]{3,2,1,0:T(2,128)(2,1)S(1)} collective-permute-done((bf16[10,6,1,256]{3,2,1,0:T(2,128)(2,1)S(1)}, bf16[10,6,1,256]{3,2,1,0:T(2,128)(2,1)S(1)}, u32[]{:S(2)}, u32[]{:S(2)}) %collective-permute-start.5) | collective-permute-done | bytes 30752 | tf_op jit(solution)/shard_map/ppermute | solution.py:14
  132.8 2.2 fusion.75
  136.3 73.2 %all-gather.2.cloned.1.call-done = bf16[2,6912,256]{2,1,0:T(8,128)(2,1)} async-done(((bf16[2,864,256]{2,1,0:T(8,128)(2,1)}), bf16[2,6912,256]{2,1,0:T(8,128)(2,1)}) %all-gather.2.cloned.1.call-update) | async-done | bytes 7077904 | tf_op jit(solution)/shard_map/all_gather | solution.py:109
  209.6 1.4 fusion.60
  210.9 1.8 fusion.59
  212.7 1.2 fusion.58
  213.9 1.2 fusion.57
  215.1 1.2 fusion.56
  216.3 1.2 fusion.55
  217.6 1.2 fusion.54
  218.8 1.1 fusion.53
  220.2 1.2 convolution_add_fusion.42
  221.9 1.2 convolution_add_fusion.39
  226.9 3.4 %collective-permute-start.6 = (bf16[1,4,16,256]{3,2,1,0:T(8,128)(2,1)S(1)}, bf16[1,4,16,256]{3,2,1,0:T(8,128)(2,1)S(1)}, u32[]{:S(2)}, u32[]{:S(2)}) collective-permute-start(bf16[1,4,16,256]{3,2,1,0:T(8,128)(2,1)S(1)} %get-tuple-element.91), channel_id=1, source_target_pairs={{0,16},{4,20},{8,24},{12,28},{1,17},{5,21},{9,25},{13,29},{2,18},{... | collective-permute-start | bytes 98312 | tf_op jit(solution)/shard_map/ppermute | solution.py:14
  230.3 1.3 fusion.50
  231.6 1.3 collective-permute-start.7
  232.9 5.7 %collective-permute-done.7 = bf16[1,4,16,256]{3,2,1,0:T(8,128)(2,1)S(1)} collective-permute-done((bf16[1,4,16,256]{3,2,1,0:T(8,128)(2,1)S(1)}, bf16[1,4,16,256]{3,2,1,0:T(8,128)(2,1)S(1)}, u32[]{:S(2)}, u32[]{:S(2)}) %collective-permute-start.7) | collective-permute-done | bytes 32800 | tf_op jit(solution)/shard_map/ppermute | solution.py:14
  238.6 2.1 collective-permute-start.8
  240.8 1.3 collective-permute-start.9
  242.8 4.3 %collective-permute-done.9 = bf16[10,1,16,256]{3,2,1,0:T(8,128)(2,1)S(1)} collective-permute-done((bf16[10,1,16,256]{3,2,1,0:T(8,128)(2,1)S(1)}, bf16[10,1,16,256]{3,2,1,0:T(8,128)(2,1)S(1)}, u32[]{:S(2)}, u32[]{:S(2)}) %collective-permute-start.9) | collective-permute-done | bytes 81952 | tf_op jit(solution)/shard_map/ppermute | solution.py:14
  247.4 2.6 collective-permute-start.10
  250.0 1.5 collective-permute-start.11
  251.5 0.8 collective-permute-done.10
  252.4 3.7 %collective-permute-done.11 = bf16[10,6,1,256]{3,2,1,0:T(2,128)(2,1)S(1)} collective-permute-done((bf16[10,6,1,256]{3,2,1,0:T(2,128)(2,1)S(1)}, bf16[10,6,1,256]{3,2,1,0:T(2,128)(2,1)S(1)}, u32[]{:S(2)}, u32[]{:S(2)}) %collective-permute-start.11) | collective-permute-done | bytes 30752 | tf_op jit(solution)/shard_map/ppermute | solution.py:14
  263.7 0.9 fusion.43
  (122 shorter events, 17.8 us)
Async XLA Ops:
  7.2 41.6 %all-reduce.4.cloned.1.call-start = ((), (), s32[]{:S(2)}) async-start(), calls=%async_computation | async-start | bytes 1769472 | tf_op jit(solution)/shard_map/psum | solution.py:77
  7.9 82.7 %all-reduce.6.cloned.1.call-start = ((), (), s32[]{:S(2)}) async-start(), calls=%async_computation.2 | async-start | bytes 1769472 | tf_op jit(solution)/shard_map/psum | solution.py:19
  14.7 83.4 %copy-start = (bf16[1,1,8,4,16,256]{5,4,3,2,1,0:T(8,128)(2,1)S(1)}, bf16[1,1,8,4,16,256]{5,4,3,2,1,0:T(8,128)(2,1)}, u32[]{:S(2)}) copy-start(bf16[1,1,8,4,16,256]{5,4,3,2,1,0:T(8,128)(2,1)} %param.6) | copy-start | bytes 786436
  54.5 155.1 %all-gather.2.cloned.1.call-start = ((), (), s32[]{:S(2)}) async-start(), calls=%async_computation.1 | async-start | bytes 7962624 | tf_op jit(solution)/shard_map/all_gather | solution.py:109
  98.1 5.9 %collective-permute-start = (bf16[1,4,16,256]{3,2,1,0:T(8,128)(2,1)S(1)}, bf16[1,4,16,256]{3,2,1,0:T(8,128)(2,1)S(1)}, u32[]{:S(2)}, u32[]{:S(2)}) collective-permute-start(bf16[1,4,16,256]{3,2,1,0:T(8,128)(2,1)S(1)} %get-tuple-element.95), channel_id=1, source_target_pairs={{0,16},{4,20},{8,24},{12,28},{1,17},{5,21},{9,25},{13,29},{2,18},{... | collective-permute-start | bytes 98312 | tf_op jit(solution)/shard_map/ppermute | solution.py:14
  102.4 6.7 %collective-permute-start.1 = (bf16[1,4,16,256]{3,2,1,0:T(8,128)(2,1)S(1)}, bf16[1,4,16,256]{3,2,1,0:T(8,128)(2,1)S(1)}, u32[]{:S(2)}, u32[]{:S(2)}) collective-permute-start(bf16[1,4,16,256]{3,2,1,0:T(8,128)(2,1)S(1)} %get-tuple-element.96), channel_id=1, source_target_pairs={{16,0},{20,4},{24,8},{28,12},{17,1},{21,5},{25,9},{29,13},{18,2},{... | collective-permute-start | bytes 98312 | tf_op jit(solution)/shard_map/ppermute | solution.py:14
  109.2 7.2 %collective-permute-start.2 = (bf16[10,1,16,256]{3,2,1,0:T(8,128)(2,1)S(1)}, bf16[10,1,16,256]{3,2,1,0:T(8,128)(2,1)S(1)}, u32[]{:S(2)}, u32[]{:S(2)}) collective-permute-start(bf16[10,1,16,256]{3,2,1,0:T(8,128)(2,1)S(1)} %get-tuple-element.87), channel_id=1, source_target_pairs={{0,8},{4,12},{8,16},{12,20},{16,24},{20,28},{1,9},{5,13},{9,17},{1... | collective-permute-start | bytes 245768 | tf_op jit(solution)/shard_map/ppermute | solution.py:14
  112.6 10.0 %collective-permute-start.3 = (bf16[10,1,16,256]{3,2,1,0:T(8,128)(2,1)S(1)}, bf16[10,1,16,256]{3,2,1,0:T(8,128)(2,1)S(1)}, u32[]{:S(2)}, u32[]{:S(2)}) collective-permute-start(bf16[10,1,16,256]{3,2,1,0:T(8,128)(2,1)S(1)} %get-tuple-element.88), channel_id=1, source_target_pairs={{8,0},{12,4},{16,8},{20,12},{24,16},{28,20},{9,1},{13,5},{17,9},{2... | collective-permute-start | bytes 245768 | tf_op jit(solution)/shard_map/ppermute | solution.py:14
  122.7 5.9 %collective-permute-start.4 = (bf16[10,6,1,256]{3,2,1,0:T(2,128)(2,1)S(1)}, bf16[10,6,1,256]{3,2,1,0:T(2,128)(2,1)S(1)}, u32[]{:S(2)}, u32[]{:S(2)}) collective-permute-start(bf16[10,6,1,256]{3,2,1,0:T(2,128)(2,1)S(1)} %get-tuple-element.68), channel_id=1, source_target_pairs={{0,4},{4,8},{8,12},{12,16},{16,20},{20,24},{24,28},{1,5},{5,9},{9,... | collective-permute-start | bytes 92168 | tf_op jit(solution)/shard_map/ppermute | solution.py:14
  126.1 6.1 %collective-permute-start.5 = (bf16[10,6,1,256]{3,2,1,0:T(2,128)(2,1)S(1)}, bf16[10,6,1,256]{3,2,1,0:T(2,128)(2,1)S(1)}, u32[]{:S(2)}, u32[]{:S(2)}) collective-permute-start(bf16[10,6,1,256]{3,2,1,0:T(2,128)(2,1)S(1)} %get-tuple-element.67), channel_id=1, source_target_pairs={{4,0},{8,4},{12,8},{16,12},{20,16},{24,20},{28,24},{5,1},{9,5},{13... | collective-permute-start | bytes 92168 | tf_op jit(solution)/shard_map/ppermute | solution.py:14
  209.5 10.4 %copy-start.1 = (bf16[2,6912,256]{2,1,0:T(8,128)(2,1)S(1)}, bf16[2,6912,256]{2,1,0:T(8,128)(2,1)}, u32[]{:S(2)}) copy-start(bf16[2,6912,256]{2,1,0:T(8,128)(2,1)} %all-gather.2.cloned.1.call-done) | copy-start | bytes 21233668
  209.5 11.8 %copy-start.15 = (bf16[8,4,16,256]{3,2,1,0:T(8,128)(2,1)S(1)}, bf16[8,4,16,256]{3,2,1,0:T(8,128)(2,1)}, u32[]{:S(2)}) copy-start(bf16[8,4,16,256]{3,2,1,0:T(8,128)(2,1)} %get-tuple-element.51) | copy-start | bytes 786436
  209.6 12.1 %copy-start.14 = (bf16[8,4,16,256]{3,2,1,0:T(8,128)(2,1)S(1)}, bf16[8,4,16,256]{3,2,1,0:T(8,128)(2,1)}, u32[]{:S(2)}) copy-start(bf16[8,4,16,256]{3,2,1,0:T(8,128)(2,1)} %get-tuple-element.106) | copy-start | bytes 786436
  209.6 13.5 %copy-start.13 = (bf16[8,4,16,256]{3,2,1,0:T(8,128)(2,1)S(1)}, bf16[8,4,16,256]{3,2,1,0:T(8,128)(2,1)}, u32[]{:S(2)}) copy-start(bf16[8,4,16,256]{3,2,1,0:T(8,128)(2,1)} %get-tuple-element.50) | copy-start | bytes 786436
  210.9 12.4 %copy-start.12 = (bf16[8,4,16,256]{3,2,1,0:T(8,128)(2,1)S(1)}, bf16[8,4,16,256]{3,2,1,0:T(8,128)(2,1)}, u32[]{:S(2)}) copy-start(bf16[8,4,16,256]{3,2,1,0:T(8,128)(2,1)} %get-tuple-element.107) | copy-start | bytes 786436
  213.9 9.6 %copy-start.4 = (bf16[8,4,16,256]{3,2,1,0:T(8,128)(2,1)S(1)}, bf16[8,4,16,256]{3,2,1,0:T(8,128)(2,1)}, u32[]{:S(2)}) copy-start(bf16[8,4,16,256]{3,2,1,0:T(8,128)(2,1)} %get-tuple-element.77) | copy-start | bytes 786436
  216.3 7.5 %copy-start.11 = (bf16[8,4,16,256]{3,2,1,0:T(8,128)(2,1)S(1)}, bf16[8,4,16,256]{3,2,1,0:T(8,128)(2,1)}, u32[]{:S(2)}) copy-start(bf16[8,4,16,256]{3,2,1,0:T(8,128)(2,1)} %get-tuple-element.49) | copy-start | bytes 786436
  217.6 6.5 %copy-start.10 = (bf16[8,4,16,256]{3,2,1,0:T(8,128)(2,1)S(1)}, bf16[8,4,16,256]{3,2,1,0:T(8,128)(2,1)}, u32[]{:S(2)}) copy-start(bf16[8,4,16,256]{3,2,1,0:T(8,128)(2,1)} %get-tuple-element.108) | copy-start | bytes 786436
  219.9 4.4 %copy-start.3 = (bf16[8,4,16,256]{3,2,1,0:T(8,128)(2,1)S(1)}, bf16[8,4,16,256]{3,2,1,0:T(8,128)(2,1)}, u32[]{:S(2)}) copy-start(bf16[8,4,16,256]{3,2,1,0:T(8,128)(2,1)} %get-tuple-element.118) | copy-start | bytes 786436
  220.2 4.4 %copy-start.9 = (bf16[8,4,16,256]{3,2,1,0:T(8,128)(2,1)S(1)}, bf16[8,4,16,256]{3,2,1,0:T(8,128)(2,1)}, u32[]{:S(2)}) copy-start(bf16[8,4,16,256]{3,2,1,0:T(8,128)(2,1)} %get-tuple-element.48) | copy-start | bytes 786436
  221.4 3.4 %copy-start.8 = (bf16[8,4,16,256]{3,2,1,0:T(8,128)(2,1)S(1)}, bf16[8,4,16,256]{3,2,1,0:T(8,128)(2,1)}, u32[]{:S(2)}) copy-start(bf16[8,4,16,256]{3,2,1,0:T(8,128)(2,1)} %get-tuple-element.109) | copy-start | bytes 786436
  223.6 1.9 copy-start.16
  223.8 1.9 copy-start.7
  224.1 1.9 copy-start.6
  224.3 1.8 copy-start.2
  224.6 1.8 copy-start.5
  226.9 6.0 %collective-permute-start.6 = (bf16[1,4,16,256]{3,2,1,0:T(8,128)(2,1)S(1)}, bf16[1,4,16,256]{3,2,1,0:T(8,128)(2,1)S(1)}, u32[]{:S(2)}, u32[]{:S(2)}) collective-permute-start(bf16[1,4,16,256]{3,2,1,0:T(8,128)(2,1)S(1)} %get-tuple-element.91), channel_id=1, source_target_pairs={{0,16},{4,20},{8,24},{12,28},{1,17},{5,21},{9,25},{13,29},{2,18},{... | collective-permute-start | bytes 98312 | tf_op jit(solution)/shard_map/ppermute | solution.py:14
  231.6 7.0 %collective-permute-start.7 = (bf16[1,4,16,256]{3,2,1,0:T(8,128)(2,1)S(1)}, bf16[1,4,16,256]{3,2,1,0:T(8,128)(2,1)S(1)}, u32[]{:S(2)}, u32[]{:S(2)}) collective-permute-start(bf16[1,4,16,256]{3,2,1,0:T(8,128)(2,1)S(1)} %get-tuple-element.92), channel_id=1, source_target_pairs={{16,0},{20,4},{24,8},{28,12},{17,1},{21,5},{25,9},{29,13},{18,2},{... | collective-permute-start | bytes 98312 | tf_op jit(solution)/shard_map/ppermute | solution.py:14
  238.6 4.2 %collective-permute-start.8 = (bf16[10,1,16,256]{3,2,1,0:T(8,128)(2,1)S(1)}, bf16[10,1,16,256]{3,2,1,0:T(8,128)(2,1)S(1)}, u32[]{:S(2)}, u32[]{:S(2)}) collective-permute-start(bf16[10,1,16,256]{3,2,1,0:T(8,128)(2,1)S(1)} %get-tuple-element.83), channel_id=1, source_target_pairs={{0,8},{4,12},{8,16},{12,20},{16,24},{20,28},{1,9},{5,13},{9,17},{1... | collective-permute-start | bytes 245768 | tf_op jit(solution)/shard_map/ppermute | solution.py:14
  240.8 6.3 %collective-permute-start.9 = (bf16[10,1,16,256]{3,2,1,0:T(8,128)(2,1)S(1)}, bf16[10,1,16,256]{3,2,1,0:T(8,128)(2,1)S(1)}, u32[]{:S(2)}, u32[]{:S(2)}) collective-permute-start(bf16[10,1,16,256]{3,2,1,0:T(8,128)(2,1)S(1)} %get-tuple-element.84), channel_id=1, source_target_pairs={{8,0},{12,4},{16,8},{20,12},{24,16},{28,20},{9,1},{13,5},{17,9},{2... | collective-permute-start | bytes 245768 | tf_op jit(solution)/shard_map/ppermute | solution.py:14
  247.4 4.9 %collective-permute-start.10 = (bf16[10,6,1,256]{3,2,1,0:T(2,128)(2,1)S(1)}, bf16[10,6,1,256]{3,2,1,0:T(2,128)(2,1)S(1)}, u32[]{:S(2)}, u32[]{:S(2)}) collective-permute-start(bf16[10,6,1,256]{3,2,1,0:T(2,128)(2,1)S(1)} %get-tuple-element.64), channel_id=1, source_target_pairs={{0,4},{4,8},{8,12},{12,16},{16,20},{20,24},{24,28},{1,5},{5,9},{9,... | collective-permute-start | bytes 92168 | tf_op jit(solution)/shard_map/ppermute | solution.py:14
  250.0 6.1 %collective-permute-start.11 = (bf16[10,6,1,256]{3,2,1,0:T(2,128)(2,1)S(1)}, bf16[10,6,1,256]{3,2,1,0:T(2,128)(2,1)S(1)}, u32[]{:S(2)}, u32[]{:S(2)}) collective-permute-start(bf16[10,6,1,256]{3,2,1,0:T(2,128)(2,1)S(1)} %get-tuple-element.63), channel_id=1, source_target_pairs={{4,0},{8,4},{12,8},{16,12},{20,16},{24,20},{28,24},{5,1},{9,5},{13... | collective-permute-start | bytes 92168 | tf_op jit(solution)/shard_map/ppermute | solution.py:14
Sparse Core Ops, SparseCore 0:
  10.3 38.3 all-reduce.3
  54.6 35.9 all-reduce.5
  98.2 111.2 all-gather.1
where the time goes:
time: 272 us; the launch traced here: 271 us
  waiting for transfers between devices  176 us (65%)
  starting transfers between devices  27.3 us (10%)
  matrix products  22.9 us (8%)
  between operations  19.8 us (7%)
  local copies, waits for them, and re-layouts  12.8 us (5%)
  other arithmetic  12.4 us (5%)
    all_gather x1, waiting for transfers between devices, shards(): lax.all_gather(new_master.astype(jnp.bfloat16), 'space', axis=1, tiled=True)  73.2 us
    psum x1, waiting for transfers between devices, spread(): return lax.psum(kept, axis)  36.1 us
    psum x1, waiting for transfers between devices, shards(): lax.psum(grad_parts[0].astype(jnp.float32).astype(jnp.bfloat16), 'rep')  34 us
    ppermute x12, waiting for transfers between devices, passed_along(): lax.ppermute(value, axis, [(source, source + steps) for source in range(f...  31.9 us
    ppermute x12, starting transfers between devices, passed_along(): lax.ppermute(value, axis, [(source, source + steps) for source in range(f...  27.2 us
    dot_general x54, matrix products, convolve(): jnp.dot(window.reshape(-1, channels), weights_tap, preferred_element_type...  22.9 us
    unnamed x42, local copies, waits for them, and re-layouts  6.87 us
  transfers between devices with their start and end apart: 15, of which 13 were waited for; matrix products, arithmetic and copies ran while one was open for 3% of the time, Pallas kernels for 0%

commit v1 on v0

--- a/solution.py
+++ b/solution.py
@@ -6,6 +6,17 @@
 GY = 2
 GZ = 2
 PANEL_ROWS = 216
+
+
+def gather_around(value, axis, dim):
+    ways = lax.axis_size(axis)
+    pieces = [value]
+    for far in range(1, ways):
+        pieces.append(
+            lax.ppermute(pieces[far - 1], axis, [(d, (d - 1) % ways) for d in range(ways)])
+        )
+    line = jnp.concatenate(pieces, axis=dim)
+    return jnp.roll(line, lax.axis_index(axis) * value.shape[dim], axis=dim)
 
 
 def passed_along(value, axis, steps):
@@ -106,7 +117,7 @@
     new_weights = lax.dynamic_slice_in_dim(
         new_master.reshape(filter_count, -1), rep_pos * share_len, share_len, 1
     )
-    filters = lax.all_gather(new_master.astype(jnp.bfloat16), "space", axis=1, tiled=True)
+    filters = gather_around(new_master.astype(jnp.bfloat16), "space", 1)
     grid = (lax.axis_size("space") // (GY * GZ), GY, GZ)
     strides = (GY * GZ, GZ, 1)
     coords = (space_pos // (GY * GZ), space_pos // GZ % GY, space_pos % GZ)

time: 272 us -> 319 us (1.17)
  starting transfers between devices: 27.3 us -> 77.1 us
  matrix products: 22.9 us -> 14.5 us
    ppermute x0 -> x7, waiting for transfers between devices: none -> 75.6 us  [gather_around(): lax.ppermute(pieces[far - 1], axis, [(d, (d - 1) % ways) for d in range(w...]
    all_gather x1 -> x0, waiting for transfers between devices: 73.2 us -> none  [shards(): lax.all_gather(new_master.astype(jnp.bfloat16), 'space', axis=1, tiled=True)]
    ppermute x0 -> x7, starting transfers between devices: none -> 49.2 us  [gather_around(): lax.ppermute(pieces[far - 1], axis, [(d, (d - 1) % ways) for d in range(w...]
    dot_general x54, matrix products: 22.9 us -> 14.5 us  [convolve(): jnp.dot(window.reshape(-1, channels), weights_tap, preferred_element_type...]
    unnamed x42 -> x25, local copies, waits for them, and re-layouts: 6.87 us -> 12.2 us
  transfers between devices with their start and end apart: 15 -> 21, of which waited for: 13 -> 14; matrix products, arithmetic and copies ran while one was open for 3% -> 3% of each run, Pallas kernels for 0% -> 0%
where the time goes in v1:
time: 319 us; the launch traced here: 317 us
  waiting for transfers between devices  178 us (56%)
  starting transfers between devices  77.1 us (24%)
  between operations  20.1 us (6%)
  local copies, waits for them, and re-layouts  15.9 us (5%)
  matrix products  14.5 us (5%)
  other arithmetic  11.7 us (4%)
    ppermute x7, waiting for transfers between devices, gather_around(): lax.ppermute(pieces[far - 1], axis, [(d, (d - 1) % ways) for d in range(w...  75.6 us
    ppermute x7, starting transfers between devices, gather_around(): lax.ppermute(pieces[far - 1], axis, [(d, (d - 1) % ways) for d in range(w...  49.2 us
    psum x1, waiting for transfers between devices, spread(): return lax.psum(kept, axis)  36.1 us
    psum x1, waiting for transfers between devices, shards(): lax.psum(grad_parts[0].astype(jnp.float32).astype(jnp.bfloat16), 'rep')  34 us
    ppermute x12, waiting for transfers between devices, passed_along(): lax.ppermute(value, axis, [(source, source + steps) for source in range(f...  31.4 us
    ppermute x12, starting transfers between devices, passed_along(): lax.ppermute(value, axis, [(source, source + steps) for source in range(f...  27.8 us
    dot_general x54, matrix products, convolve(): jnp.dot(window.reshape(-1, channels), weights_tap, preferred_element_type...  14.5 us
    unnamed x25, local copies, waits for them, and re-layouts  12.2 us
  transfers between devices with their start and end apart: 21, of which 14 were waited for; matrix products, arithmetic and copies ran while one was open for 3% of the time, Pallas kernels for 0%

profile of v1, /device:TPU:0, one launch (start us, length us, event | category | flops | bytes accessed | tf_op | source)
XLA Modules:
  0.0 317.0 jit_solution(13571468652632524587)
XLA Ops:
  14.7 34.0 %all-reduce.4.cloned.1.call-done = bf16[2,864,256]{2,1,0:T(8,128)(2,1)} async-done(((bf16[2,864,256]{2,1,0:T(8,128)(2,1)}), bf16[2,864,256]{2,1,0:T(8,128)(2,1)}) %all-reduce.4.cloned.1.call-update) | async-done | bytes 884752 | tf_op jit(solution)/shard_map/psum | solution.py:88
  48.7 4.8 %fusion.8 = (f32[1,2,864,256]{3,2,1,0:T(8,128)}, bf16[2,864,256]{2,1,0:T(8,128)(2,1)S(1)}, f32[1,2,864,256]{3,2,1,0:T(8,128)}) fusion(bf16[2,864,256]{2,1,0:T(8,128)(2,1)} %all-reduce.4.cloned.1.call-done, f32[1,2,864,256]{3,2,1,0:T(8,128)} %param.10, pred[2,864]{1,0:T(4,128)(4,1)S(1)} %eq.54, f32[2,864,256]{2,1,0:T(8,128)} %param.8, f32[1,2,864,256]{3,2,1,0:T(8,128)} %param.9), kind=kLoop, calls=%fused_computation.12 | loop fusion | flops 8404992 | bytes 10618560 | tf_op jit(solution)/shard_map/broadcast_in_dim | solution.py:97
  53.6 0.9 fusion.147
  54.5 36.1 %all-reduce.6.cloned.1.call-done = (bf16[216,256]{1,0:T(8,128)(2,1)}, bf16[216,256]{1,0:T(8,128)(2,1)}, bf16[216,256]{1,0:T(8,128)(2,1)}, bf16[216,256]{1,0:T(8,...) async-done(((bf16[216,256]{1,0:T(8,128)(2,1)}, bf16[216,256]{1,0:T(8,128)(2,1)}, ...) | async-done | bytes 884752 | tf_op jit(solution)/shard_map/psum | solution.py:30
  90.6 0.9 constant_dynamic-update-slice_fusion.7
  91.5 0.9 constant_dynamic-update-slice_fusion.3
  92.4 0.9 constant_dynamic-update-slice_fusion.6
  93.3 0.9 constant_dynamic-update-slice_fusion.5
  94.2 0.9 constant_dynamic-update-slice_fusion.2
  95.1 0.9 constant_dynamic-update-slice_fusion.1
  96.0 1.0 constant_dynamic-update-slice_fusion
  97.0 1.0 pad_maximum_fusion
  98.1 4.2 %collective-permute-start.5 = (bf16[2,864,256]{2,1,0:T(8,128)(2,1)S(1)}, bf16[2,864,256]{2,1,0:T(8,128)(2,1)S(1)}, u32[]{:S(2)}, u32[]{:S(2)}) collective-permute-start(bf16[2,864,256]{2,1,0:T(8,128)(2,1)S(1)} %get-tuple-element.17), channel_id=1, source_target_pairs={{0,28},{4,0},{8,4},{12,8},{16,12},{20,16},{24,20},{28,24},{1,29},{... | collective-permute-start | bytes 2654216 | tf_op jit(solution)/shard_map/ppermute | solution.py:16
  102.3 18.0 %collective-permute-done.5 = bf16[2,864,256]{2,1,0:T(8,128)(2,1)S(1)} collective-permute-done((bf16[2,864,256]{2,1,0:T(8,128)(2,1)S(1)}, bf16[2,864,256]{2,1,0:T(8,128)(2,1)S(1)}, u32[]{:S(2)}, u32[]{:S(2)}) %collective-permute-start.5) | collective-permute-done | bytes 884768 | tf_op jit(solution)/shard_map/ppermute | solution.py:16
  120.2 5.2 %collective-permute-start.6 = (bf16[2,864,256]{2,1,0:T(8,128)(2,1)S(1)}, bf16[2,864,256]{2,1,0:T(8,128)(2,1)S(1)}, u32[]{:S(2)}, u32[]{:S(2)}) collective-permute-start(bf16[2,864,256]{2,1,0:T(8,128)(2,1)S(1)} %collective-permute-done.5), channel_id=1, source_target_pairs={{0,28},{4,0},{8,4},{12,8},{16,12},{20,16},{24,20},{28,24},{1,29},{... | collective-permute-start | bytes 2654216 | tf_op jit(solution)/shard_map/ppermute | solution.py:16
  125.4 17.1 %collective-permute-done.6 = bf16[2,864,256]{2,1,0:T(8,128)(2,1)S(1)} collective-permute-done((bf16[2,864,256]{2,1,0:T(8,128)(2,1)S(1)}, bf16[2,864,256]{2,1,0:T(8,128)(2,1)S(1)}, u32[]{:S(2)}, u32[]{:S(2)}) %collective-permute-start.6) | collective-permute-done | bytes 884768 | tf_op jit(solution)/shard_map/ppermute | solution.py:16
  142.5 5.2 %collective-permute-start.7 = (bf16[2,864,256]{2,1,0:T(8,128)(2,1)S(1)}, bf16[2,864,256]{2,1,0:T(8,128)(2,1)}, u32[]{:S(2)}, u32[]{:S(2)}) collective-permute-start(bf16[2,864,256]{2,1,0:T(8,128)(2,1)S(1)} %collective-permute-done.6), channel_id=1, source_target_pairs={{0,28},{4,0},{8,4},{12,8},{16,12},{20,16},{24,20},{28,24},{1,29},{... | collective-permute-start | bytes 2654216 | tf_op jit(solution)/shard_map/ppermute | solution.py:16
  147.7 16.2 %collective-permute-done.7 = bf16[2,864,256]{2,1,0:T(8,128)(2,1)} collective-permute-done((bf16[2,864,256]{2,1,0:T(8,128)(2,1)S(1)}, bf16[2,864,256]{2,1,0:T(8,128)(2,1)}, u32[]{:S(2)}, u32[]{:S(2)}) %collective-permute-start.7) | collective-permute-done | bytes 884768 | tf_op jit(solution)/shard_map/ppermute | solution.py:16
  164.0 5.4 %collective-permute-start.8 = (bf16[2,864,256]{2,1,0:T(8,128)(2,1)}, bf16[2,864,256]{2,1,0:T(8,128)(2,1)}, u32[]{:S(2)}, u32[]{:S(2)}) collective-permute-start(bf16[2,864,256]{2,1,0:T(8,128)(2,1)} %collective-permute-done.7), channel_id=1, source_target_pairs={{0,28},{4,0},{8,4},{12,8},{16,12},{20,16},{24,20},{28,24},{1,29},{... | collective-permute-start | bytes 2654216 | tf_op jit(solution)/shard_map/ppermute | solution.py:16
  169.3 1.3 collective-permute-start
  170.6 1.3 collective-permute-start.1
  172.0 15.0 %collective-permute-done = bf16[1,4,16,256]{3,2,1,0:T(8,128)(2,1)S(1)} collective-permute-done((bf16[1,4,16,256]{3,2,1,0:T(8,128)(2,1)S(1)}, bf16[1,4,16,256]{3,2,1,0:T(8,128)(2,1)S(1)}, u32[]{:S(2)}, u32[]{:S(2)}) %collective-permute-start) | collective-permute-done | bytes 32800 | tf_op jit(solution)/shard_map/ppermute | solution.py:25
  187.1 1.3 collective-permute-start.2
  188.4 1.3 collective-permute-start.3
  189.7 2.0 collective-permute-start.9
  191.7 6.5 %collective-permute-done.3 = bf16[10,1,16,256]{3,2,1,0:T(8,128)(2,1)S(1)} collective-permute-done((bf16[10,1,16,256]{3,2,1,0:T(8,128)(2,1)S(1)}, bf16[10,1,16,256]{3,2,1,0:T(8,128)(2,1)S(1)}, u32[]{:S(2)}, u32[]{:S(2)}) %collective-permute-start.3) | collective-permute-done | bytes 81952 | tf_op jit(solution)/shard_map/ppermute | solution.py:25
  198.3 1.3 collective-permute-start.12
  199.6 4.5 %collective-permute-start.4 = (bf16[10,6,1,256]{3,2,1,0:T(2,128)(2,1)S(1)}, bf16[10,6,1,256]{3,2,1,0:T(2,128)(2,1)S(1)}, u32[]{:S(2)}, u32[]{:S(2)}) collective-permute-start(bf16[10,6,1,256]{3,2,1,0:T(2,128)(2,1)S(1)} %get-tuple-element.69), channel_id=1, source_target_pairs={{0,4},{4,8},{8,12},{12,16},{16,20},{20,24},{24,28},{1,5},{5,9},{9,... | collective-permute-start | bytes 92168 | tf_op jit(solution)/shard_map/ppermute | solution.py:25
  204.4 2.9 collective-permute-done.9
  207.4 18.7 %collective-permute-start.10 = (bf16[2,864,256]{2,1,0:T(8,128)(2,1)S(1)}, bf16[2,864,256]{2,1,0:T(8,128)(2,1)S(1)}, u32[]{:S(2)}, u32[]{:S(2)}) collective-permute-start(bf16[2,864,256]{2,1,0:T(8,128)(2,1)S(1)} %collective-permute-done.9), channel_id=1, source_target_pairs={{0,28},{4,0},{8,4},{12,8},{16,12},{20,16},{24,20},{28,24},{1,29},{... | collective-permute-start | bytes 2654216 | tf_op jit(solution)/shard_map/ppermute | solution.py:16
  228.9 14.4 %collective-permute-done.10 = bf16[2,864,256]{2,1,0:T(8,128)(2,1)S(1)} collective-permute-done((bf16[2,864,256]{2,1,0:T(8,128)(2,1)S(1)}, bf16[2,864,256]{2,1,0:T(8,128)(2,1)S(1)}, u32[]{:S(2)}, u32[]{:S(2)}) %collective-permute-start.10) | collective-permute-done | bytes 884768 | tf_op jit(solution)/shard_map/ppermute | solution.py:16
  243.3 8.6 %collective-permute-start.11 = (bf16[2,864,256]{2,1,0:T(8,128)(2,1)S(1)}, bf16[2,864,256]{2,1,0:T(8,128)(2,1)S(1)}, u32[]{:S(2)}, u32[]{:S(2)}) collective-permute-start(bf16[2,864,256]{2,1,0:T(8,128)(2,1)S(1)} %collective-permute-done.10), channel_id=1, source_target_pairs={{0,28},{4,0},{8,4},{12,8},{16,12},{20,16},{24,20},{28,24},{1,29},{... | collective-permute-start | bytes 2654216 | tf_op jit(solution)/shard_map/ppermute | solution.py:16
  251.9 1.3 fusion.92
  253.3 1.2 constant_dynamic-update-slice_fusion.20
  254.5 1.2 constant_dynamic-update-slice_fusion.19
  255.9 6.9 %collective-permute-done.11 = bf16[2,864,256]{2,1,0:T(8,128)(2,1)S(1)} collective-permute-done((bf16[2,864,256]{2,1,0:T(8,128)(2,1)S(1)}, bf16[2,864,256]{2,1,0:T(8,128)(2,1)S(1)}, u32[]{:S(2)}, u32[]{:S(2)}) %collective-permute-start.11) | collective-permute-done | bytes 884768 | tf_op jit(solution)/shard_map/ppermute | solution.py:16
  263.1 1.2 constant_dynamic-update-slice_fusion.12
  264.3 1.2 constant_dynamic-update-slice_fusion.11
  272.0 1.1 fusion.60
  273.3 2.1 collective-permute-start.13
  275.4 1.3 collective-permute-start.14
  277.0 5.1 %collective-permute-done.14 = bf16[1,4,16,256]{3,2,1,0:T(8,128)(2,1)S(1)} collective-permute-done((bf16[1,4,16,256]{3,2,1,0:T(8,128)(2,1)S(1)}, bf16[1,4,16,256]{3,2,1,0:T(8,128)(2,1)S(1)}, u32[]{:S(2)}, u32[]{:S(2)}) %collective-permute-start.14) | collective-permute-done | bytes 32800 | tf_op jit(solution)/shard_map/ppermute | solution.py:25
  282.2 3.3 %collective-permute-start.15 = (bf16[10,1,16,256]{3,2,1,0:T(8,128)(2,1)S(1)}, bf16[10,1,16,256]{3,2,1,0:T(8,128)(2,1)S(1)}, u32[]{:S(2)}, u32[]{:S(2)}) collective-permute-start(bf16[10,1,16,256]{3,2,1,0:T(8,128)(2,1)S(1)} %get-tuple-element.85), channel_id=1, source_target_pairs={{0,8},{4,12},{8,16},{12,20},{16,24},{20,28},{1,9},{5,13},{9,17},{1... | collective-permute-start | bytes 245768 | tf_op jit(solution)/shard_map/ppermute | solution.py:25
  285.4 1.5 collective-permute-start.16
  287.5 4.3 %collective-permute-done.16 = bf16[10,1,16,256]{3,2,1,0:T(8,128)(2,1)S(1)} collective-permute-done((bf16[10,1,16,256]{3,2,1,0:T(8,128)(2,1)S(1)}, bf16[10,1,16,256]{3,2,1,0:T(8,128)(2,1)S(1)}, u32[]{:S(2)}, u32[]{:S(2)}) %collective-permute-start.16) | collective-permute-done | bytes 81952 | tf_op jit(solution)/shard_map/ppermute | solution.py:25
  292.3 1.3 collective-permute-start.18
  293.6 7.4 %collective-permute-start.17 = (bf16[10,6,1,256]{3,2,1,0:T(2,128)(2,1)S(1)}, bf16[10,6,1,256]{3,2,1,0:T(2,128)(2,1)S(1)}, u32[]{:S(2)}, u32[]{:S(2)}) collective-permute-start(bf16[10,6,1,256]{3,2,1,0:T(2,128)(2,1)S(1)} %get-tuple-element.65), channel_id=1, source_target_pairs={{0,4},{4,8},{8,12},{12,16},{16,20},{20,24},{24,28},{1,5},{5,9},{9,... | collective-permute-start | bytes 92168 | tf_op jit(solution)/shard_map/ppermute | solution.py:25
  308.2 1.1 fusion.54
  (118 shorter events, 21.8 us)
Async XLA Ops:
  7.2 162.2 %copy-start = (bf16[1,1,8,4,16,256]{5,4,3,2,1,0:T(8,128)(2,1)S(1)}, bf16[1,1,8,4,16,256]{5,4,3,2,1,0:T(8,128)(2,1)}, u32[]{:S(2)}) copy-start(bf16[1,1,8,4,16,256]{5,4,3,2,1,0:T(8,128)(2,1)} %param.6) | copy-start | bytes 786436
  7.2 41.6 %all-reduce.4.cloned.1.call-start = ((), (), s32[]{:S(2)}) async-start(), calls=%async_computation | async-start | bytes 1769472 | tf_op jit(solution)/shard_map/psum | solution.py:88
  7.9 82.7 %all-reduce.6.cloned.1.call-start = ((), (), s32[]{:S(2)}) async-start(), calls=%async_computation.1 | async-start | bytes 1769472 | tf_op jit(solution)/shard_map/psum | solution.py:30
  98.1 22.2 %collective-permute-start.5 = (bf16[2,864,256]{2,1,0:T(8,128)(2,1)S(1)}, bf16[2,864,256]{2,1,0:T(8,128)(2,1)S(1)}, u32[]{:S(2)}, u32[]{:S(2)}) collective-permute-start(bf16[2,864,256]{2,1,0:T(8,128)(2,1)S(1)} %get-tuple-element.17), channel_id=1, source_target_pairs={{0,28},{4,0},{8,4},{12,8},{16,12},{20,16},{24,20},{28,24},{1,29},{... | collective-permute-start | bytes 2654216 | tf_op jit(solution)/shard_map/ppermute | solution.py:16
  120.2 22.3 %collective-permute-start.6 = (bf16[2,864,256]{2,1,0:T(8,128)(2,1)S(1)}, bf16[2,864,256]{2,1,0:T(8,128)(2,1)S(1)}, u32[]{:S(2)}, u32[]{:S(2)}) collective-permute-start(bf16[2,864,256]{2,1,0:T(8,128)(2,1)S(1)} %collective-permute-done.5), channel_id=1, source_target_pairs={{0,28},{4,0},{8,4},{12,8},{16,12},{20,16},{24,20},{28,24},{1,29},{... | collective-permute-start | bytes 2654216 | tf_op jit(solution)/shard_map/ppermute | solution.py:16
  142.5 21.4 %collective-permute-start.7 = (bf16[2,864,256]{2,1,0:T(8,128)(2,1)S(1)}, bf16[2,864,256]{2,1,0:T(8,128)(2,1)}, u32[]{:S(2)}, u32[]{:S(2)}) collective-permute-start(bf16[2,864,256]{2,1,0:T(8,128)(2,1)S(1)} %collective-permute-done.6), channel_id=1, source_target_pairs={{0,28},{4,0},{8,4},{12,8},{16,12},{20,16},{24,20},{28,24},{1,29},{... | collective-permute-start | bytes 2654216 | tf_op jit(solution)/shard_map/ppermute | solution.py:16
  164.0 25.8 %collective-permute-start.8 = (bf16[2,864,256]{2,1,0:T(8,128)(2,1)}, bf16[2,864,256]{2,1,0:T(8,128)(2,1)}, u32[]{:S(2)}, u32[]{:S(2)}) collective-permute-start(bf16[2,864,256]{2,1,0:T(8,128)(2,1)} %collective-permute-done.7), channel_id=1, source_target_pairs={{0,28},{4,0},{8,4},{12,8},{16,12},{20,16},{24,20},{28,24},{1,29},{... | collective-permute-start | bytes 2654216 | tf_op jit(solution)/shard_map/ppermute | solution.py:16
  169.3 17.7 %collective-permute-start = (bf16[1,4,16,256]{3,2,1,0:T(8,128)(2,1)S(1)}, bf16[1,4,16,256]{3,2,1,0:T(8,128)(2,1)S(1)}, u32[]{:S(2)}, u32[]{:S(2)}) collective-permute-start(bf16[1,4,16,256]{3,2,1,0:T(8,128)(2,1)S(1)} %get-tuple-element.97), channel_id=1, source_target_pairs={{0,16},{4,20},{8,24},{12,28},{1,17},{5,21},{9,25},{13,29},{2,18},{... | collective-permute-start | bytes 98312 | tf_op jit(solution)/shard_map/ppermute | solution.py:25
  170.6 16.4 %collective-permute-start.1 = (bf16[1,4,16,256]{3,2,1,0:T(8,128)(2,1)S(1)}, bf16[1,4,16,256]{3,2,1,0:T(8,128)(2,1)S(1)}, u32[]{:S(2)}, u32[]{:S(2)}) collective-permute-start(bf16[1,4,16,256]{3,2,1,0:T(8,128)(2,1)S(1)} %get-tuple-element.98), channel_id=1, source_target_pairs={{16,0},{20,4},{24,8},{28,12},{17,1},{21,5},{25,9},{29,13},{18,2},{... | collective-permute-start | bytes 98312 | tf_op jit(solution)/shard_map/ppermute | solution.py:25
  172.0 81.2 %copy-start.1 = (bf16[2,13824,256]{2,1,0:T(8,128)(2,1)S(1)}, bf16[2,13824,256]{2,1,0:T(8,128)(2,1)}, u32[]{:S(2)}) copy-start(bf16[2,13824,256]{2,1,0:T(8,128)(2,1)} %get-tuple-element.18) | copy-start | bytes 42467332
  187.1 4.6 %collective-permute-start.2 = (bf16[10,1,16,256]{3,2,1,0:T(8,128)(2,1)S(1)}, bf16[10,1,16,256]{3,2,1,0:T(8,128)(2,1)S(1)}, u32[]{:S(2)}, u32[]{:S(2)}) collective-permute-start(bf16[10,1,16,256]{3,2,1,0:T(8,128)(2,1)S(1)} %get-tuple-element.89), channel_id=1, source_target_pairs={{0,8},{4,12},{8,16},{12,20},{16,24},{20,28},{1,9},{5,13},{9,17},{1... | collective-permute-start | bytes 245768 | tf_op jit(solution)/shard_map/ppermute | solution.py:25
  188.4 9.8 %collective-permute-start.3 = (bf16[10,1,16,256]{3,2,1,0:T(8,128)(2,1)S(1)}, bf16[10,1,16,256]{3,2,1,0:T(8,128)(2,1)S(1)}, u32[]{:S(2)}, u32[]{:S(2)}) collective-permute-start(bf16[10,1,16,256]{3,2,1,0:T(8,128)(2,1)S(1)} %get-tuple-element.90), channel_id=1, source_target_pairs={{8,0},{12,4},{16,8},{20,12},{24,16},{28,20},{9,1},{13,5},{17,9},{2... | collective-permute-start | bytes 245768 | tf_op jit(solution)/shard_map/ppermute | solution.py:25
  189.7 17.6 %collective-permute-start.9 = (bf16[2,864,256]{2,1,0:T(8,128)(2,1)}, bf16[2,864,256]{2,1,0:T(8,128)(2,1)S(1)}, u32[]{:S(2)}, u32[]{:S(2)}) collective-permute-start(bf16[2,864,256]{2,1,0:T(8,128)(2,1)} %collective-permute-done.8), channel_id=1, source_target_pairs={{0,28},{4,0},{8,4},{12,8},{16,12},{20,16},{24,20},{28,24},{1,29},{... | collective-permute-start | bytes 2654216 | tf_op jit(solution)/shard_map/ppermute | solution.py:16
  198.3 27.8 %collective-permute-start.12 = (bf16[10,6,1,256]{3,2,1,0:T(2,128)(2,1)S(1)}, bf16[10,6,1,256]{3,2,1,0:T(2,128)(2,1)S(1)}, u32[]{:S(2)}, u32[]{:S(2)}) collective-permute-start(bf16[10,6,1,256]{3,2,1,0:T(2,128)(2,1)S(1)} %get-tuple-element.70), channel_id=1, source_target_pairs={{4,0},{8,4},{12,8},{16,12},{20,16},{24,20},{28,24},{5,1},{9,5},{13... | collective-permute-start | bytes 92168 | tf_op jit(solution)/shard_map/ppermute | solution.py:25
  199.6 26.5 %collective-permute-start.4 = (bf16[10,6,1,256]{3,2,1,0:T(2,128)(2,1)S(1)}, bf16[10,6,1,256]{3,2,1,0:T(2,128)(2,1)S(1)}, u32[]{:S(2)}, u32[]{:S(2)}) collective-permute-start(bf16[10,6,1,256]{3,2,1,0:T(2,128)(2,1)S(1)} %get-tuple-element.69), channel_id=1, source_target_pairs={{0,4},{4,8},{8,12},{12,16},{16,20},{20,24},{24,28},{1,5},{5,9},{9,... | collective-permute-start | bytes 92168 | tf_op jit(solution)/shard_map/ppermute | solution.py:25
  207.4 35.9 %collective-permute-start.10 = (bf16[2,864,256]{2,1,0:T(8,128)(2,1)S(1)}, bf16[2,864,256]{2,1,0:T(8,128)(2,1)S(1)}, u32[]{:S(2)}, u32[]{:S(2)}) collective-permute-start(bf16[2,864,256]{2,1,0:T(8,128)(2,1)S(1)} %collective-permute-done.9), channel_id=1, source_target_pairs={{0,28},{4,0},{8,4},{12,8},{16,12},{20,16},{24,20},{28,24},{1,29},{... | collective-permute-start | bytes 2654216 | tf_op jit(solution)/shard_map/ppermute | solution.py:16
  243.3 19.6 %collective-permute-start.11 = (bf16[2,864,256]{2,1,0:T(8,128)(2,1)S(1)}, bf16[2,864,256]{2,1,0:T(8,128)(2,1)S(1)}, u32[]{:S(2)}, u32[]{:S(2)}) collective-permute-start(bf16[2,864,256]{2,1,0:T(8,128)(2,1)S(1)} %collective-permute-done.10), channel_id=1, source_target_pairs={{0,28},{4,0},{8,4},{12,8},{16,12},{20,16},{24,20},{28,24},{1,29},{... | collective-permute-start | bytes 2654216 | tf_op jit(solution)/shard_map/ppermute | solution.py:16
  273.3 3.7 %collective-permute-start.13 = (bf16[1,4,16,256]{3,2,1,0:T(8,128)(2,1)S(1)}, bf16[1,4,16,256]{3,2,1,0:T(8,128)(2,1)S(1)}, u32[]{:S(2)}, u32[]{:S(2)}) collective-permute-start(bf16[1,4,16,256]{3,2,1,0:T(8,128)(2,1)S(1)} %get-tuple-element.93), channel_id=1, source_target_pairs={{0,16},{4,20},{8,24},{12,28},{1,17},{5,21},{9,25},{13,29},{2,18},{... | collective-permute-start | bytes 98312 | tf_op jit(solution)/shard_map/ppermute | solution.py:25
  275.4 6.7 %collective-permute-start.14 = (bf16[1,4,16,256]{3,2,1,0:T(8,128)(2,1)S(1)}, bf16[1,4,16,256]{3,2,1,0:T(8,128)(2,1)S(1)}, u32[]{:S(2)}, u32[]{:S(2)}) collective-permute-start(bf16[1,4,16,256]{3,2,1,0:T(8,128)(2,1)S(1)} %get-tuple-element.94), channel_id=1, source_target_pairs={{16,0},{20,4},{24,8},{28,12},{17,1},{21,5},{25,9},{29,13},{18,2},{... | collective-permute-start | bytes 98312 | tf_op jit(solution)/shard_map/ppermute | solution.py:25
  282.2 5.3 %collective-permute-start.15 = (bf16[10,1,16,256]{3,2,1,0:T(8,128)(2,1)S(1)}, bf16[10,1,16,256]{3,2,1,0:T(8,128)(2,1)S(1)}, u32[]{:S(2)}, u32[]{:S(2)}) collective-permute-start(bf16[10,1,16,256]{3,2,1,0:T(8,128)(2,1)S(1)} %get-tuple-element.85), channel_id=1, source_target_pairs={{0,8},{4,12},{8,16},{12,20},{16,24},{20,28},{1,9},{5,13},{9,17},{1... | collective-permute-start | bytes 245768 | tf_op jit(solution)/shard_map/ppermute | solution.py:25
  285.4 6.3 %collective-permute-start.16 = (bf16[10,1,16,256]{3,2,1,0:T(8,128)(2,1)S(1)}, bf16[10,1,16,256]{3,2,1,0:T(8,128)(2,1)S(1)}, u32[]{:S(2)}, u32[]{:S(2)}) collective-permute-start(bf16[10,1,16,256]{3,2,1,0:T(8,128)(2,1)S(1)} %get-tuple-element.86), channel_id=1, source_target_pairs={{8,0},{12,4},{16,8},{20,12},{24,16},{28,20},{9,1},{13,5},{17,9},{2... | collective-permute-start | bytes 245768 | tf_op jit(solution)/shard_map/ppermute | solution.py:25
  292.3 10.0 %collective-permute-start.18 = (bf16[10,6,1,256]{3,2,1,0:T(2,128)(2,1)S(1)}, bf16[10,6,1,256]{3,2,1,0:T(2,128)(2,1)S(1)}, u32[]{:S(2)}, u32[]{:S(2)}) collective-permute-start(bf16[10,6,1,256]{3,2,1,0:T(2,128)(2,1)S(1)} %get-tuple-element.66), channel_id=1, source_target_pairs={{4,0},{8,4},{12,8},{16,12},{20,16},{24,20},{28,24},{5,1},{9,5},{13... | collective-permute-start | bytes 92168 | tf_op jit(solution)/shard_map/ppermute | solution.py:25
  293.6 9.2 %collective-permute-start.17 = (bf16[10,6,1,256]{3,2,1,0:T(2,128)(2,1)S(1)}, bf16[10,6,1,256]{3,2,1,0:T(2,128)(2,1)S(1)}, u32[]{:S(2)}, u32[]{:S(2)}) collective-permute-start(bf16[10,6,1,256]{3,2,1,0:T(2,128)(2,1)S(1)} %get-tuple-element.65), channel_id=1, source_target_pairs={{0,4},{4,8},{8,12},{12,16},{16,20},{20,24},{24,28},{1,5},{5,9},{9,... | collective-permute-start | bytes 92168 | tf_op jit(solution)/shard_map/ppermute | solution.py:25
Sparse Core Ops, SparseCore 0:
  10.4 38.3 all-reduce.3
  54.6 35.9 all-reduce.5
